TPU v7x, 512 devices: a whole 4x8x8 slice. The times are simulated.
512 devices in a mesh: bank: 8 (over x, core), gal: 64 (over z, y).
Axes of the slice: x: 4, y: 8, z: 8, core: 2. Of those that a mesh axis runs over, the one named last changes fastest.
Arguments:
- bank_queries: bfloat16 [4096, 768], P(('bank', 'gal'))
- gallery: bfloat16 [262144, 768], P('gal')
- test_queries: bfloat16 [2048, 768], P(('bank', 'gal'))
- test_slabs: int32 [2048, 8], P('bank'), may hold values from 0 to 63, all different within a row; in each aligned block of 4 rows (0 to 3, 4 to 7, ...) at most 2 rows name the same one
- test_offsets: int32 [2048, 8], P('bank'), may hold values from 0 to 31
Outputs:
- pooled: float32 [2048, 768], P(('bank', 'gal'))
Inputs may be any that keep to these rules, and one draw needn't show every extreme that they name: `test_slabs`: each row names 8 different slabs; the 4 rows of one device name no slab more than 2 times, and on some devices one slab exactly 2 times.
All inputs are finite; a program needn't handle non-finite values.
Results may differ from a plain program's by a relative error of at most 0.0065.
Values may be sent and summed in bfloat16 or wider, within the bound.
A program may use at most 64 MiB of HBM per device.

v0:
```python
import jax
import jax.numpy as jnp
from jax import lax
from jax.sharding import PartitionSpec as P

BLOCK = 128
SHARPNESS = 20.0
epsilon = 1e-06


def row_scale(matrix):
    values = matrix.astype(jnp.float32)
    return lax.rsqrt(jnp.sum(values * values, axis=1) + epsilon)


def inner_rows(first_rows, second_rows):
    return lax.dot_general(
        first_rows, second_rows, (((1,), (1,)), ((), ())), preferred_element_type=jnp.float32
    )


def body(bank_queries, gallery, test_queries, test_slabs, test_offsets):
    gallery_rows = gallery.shape[0]
    gallery_scale = row_scale(gallery)
    portion = lax.all_gather(bank_queries, "gal", axis=0, tiled=True)
    scores = (
        SHARPNESS
        * inner_rows(portion, gallery)
        * row_scale(portion)[:, None]
        * gallery_scale[None, :]
    )
    partial_sums = jnp.sum(jnp.exp(scores), axis=0)
    colsum = lax.psum(partial_sums, "bank")
    log_col = jnp.log(colsum)
    own_rows = test_queries.shape[0]
    slab_index = lax.axis_index("gal")
    queries = lax.all_gather(test_queries, "gal", axis=0, tiled=True)
    blocks_here = gallery_rows // BLOCK
    local_blocks = jnp.arange(blocks_here, dtype=jnp.int32)
    block_hits = (test_slabs == slab_index)[:, :, None] & (
        test_offsets[:, :, None] == local_blocks[None, None, :]
    )
    listed = jnp.any(block_hits, axis=1)
    row_mask = jnp.repeat(listed, BLOCK, axis=1)
    logits = (
        SHARPNESS
        * inner_rows(queries, gallery)
        * row_scale(queries)[:, None]
        * gallery_scale[None, :]
        - log_col[None, :]
    )
    weights = jnp.where(row_mask, jnp.exp(logits), jnp.float32(0.0))
    numerator = jnp.dot(weights.astype(jnp.bfloat16), gallery, preferred_element_type=jnp.float32)
    numerator, denominator = (numerator, jnp.sum(weights, axis=1))
    numer_all, denom_all = lax.psum((numerator, denominator), "gal")
    offset = slab_index * own_rows
    numer_own = lax.dynamic_slice_in_dim(numer_all, offset, own_rows, 0)
    denom_own = lax.dynamic_slice_in_dim(denom_all, offset, own_rows, 0)
    return numer_own / denom_own[:, None]


def solution(mesh):
    in_specs = (
        P(("bank", "gal"), None),
        P("gal", None),
        P(("bank", "gal"), None),
        P("bank", None),
        P("bank", None),
    )
    out_specs = P(("bank", "gal"), None)
    return jax.shard_map(body, mesh=mesh, in_specs=in_specs, out_specs=out_specs, check_vma=False)
```

profile of v0, /device:TPU:2, one launch (start us, length us, event | category | flops | bytes accessed | tf_op | source)
XLA Modules:
  0.0 317.6 jit_solution(15684312714763030671)
XLA Ops:
  6.5 0.0 copy-start.1
  6.5 0.0 copy-start.2
  6.5 0.0 copy-start.3
  6.5 0.0 copy-start
  6.5 0.0 all-reduce.2.cloned.1.call-start
  6.6 4.1 %multiply_reduce_fusion = f32[4096]{0:T(1024)S(1)} fusion(bf16[4096,768]{1,0:T(8,128)(2,1)} %param.6), kind=kLoop, calls=%fused_computation | loop fusion | flops 9433088 | bytes 6307840 | tf_op jit(solution)/shard_map/reduce_sum | solution.py:13
  10.7 0.0 copy-done.1
  10.7 0.0 copy-done.2
  10.8 0.1 copy.10
  10.9 0.0 copy-done.3
  10.9 56.8 %all-gather = bf16[64,4,768]{2,1,0:T(4,128)(2,1)S(1)} all-gather(bf16[1,4,768]{2,1,0:T(4,128)(2,1)S(1)} %bitcast.13), channel_id=1, replica_groups=mesh['bank'=8,'gal'=64] {'gal'}, dimensions={0}, use_global_device_ids=true | all-gather | bytes 399360 | tf_op jit(solution)/shard_map/all_gather | solution.py:37
  67.7 0.1 reshape.21
  67.8 0.2 multiply_reduce_fusion.2
  68.0 0.0 copy-done
  68.0 48.5 %all_gather.7 = bf16[512,768]{1,0:T(8,128)(2,1)S(1)} all-gather(bf16[8,768]{1,0:T(8,128)(2,1)S(1)} %copy-done), channel_id=1, replica_groups=mesh['bank'=8,'gal'=64] {'gal'}, dimensions={0}, use_global_device_ids=true | all-gather | bytes 798720 | tf_op jit(solution)/shard_map/all_gather | solution.py:25
  116.5 0.2 multiply_reduce_fusion.1
  116.8 6.5 %exponential_reduce_fusion = f32[4096]{0:T(1024)S(1)} fusion(bf16[512,768]{1,0:T(8,128)(2,1)S(1)} %all_gather.7, bf16[4096,768]{1,0:T(8,128)(2,1)} %param.6, f32[4096]{0:T(1024)S(1)} %add_rsqrt_fusion, f32[512]{0:T(512)S(1)} %rsqrt_multiply_fusion), kind=kOutput, calls=%fused_computation.1 | convolution fusion | flops 3227512832 | bytes 7112704 | tf_op jit(solution)/shard_map/dot_general | solution.py:17
  123.3 20.6 %psum.21 = f32[4096]{0:T(1024)S(1)} all-reduce(f32[4096]{0:T(1024)S(1)} %exponential_reduce_fusion), channel_id=1, replica_groups=mesh['bank'=8,'gal'=64] {'bank'}, use_global_device_ids=true, to_apply=%region_5.0 | all-reduce | flops 4096 | bytes 32768 | tf_op jit(solution)/shard_map/psum | solution.py:33
  143.9 0.0 slice-start
  143.9 2.1 broadcast_in_dim.5
  146.0 0.0 slice-start.1
  146.0 5.3 %fusion.8 = (f32[256]{0:T(256)S(1)}, bf16[256,4096]{1,0:T(8,128)(2,1)S(1)}) fusion(f32[4096]{0:T(1024)S(1)} %log.3, f32[4096]{0:T(1024)S(1)} %add_rsqrt_fusion, f32[256]{0:T(256)S(1)} %rsqrt_multiply_fusion.1, bf16[256,768]{1,0:T(8,128)(2,1)S(1)} %reshape.21, bf16[4096,768]{1,0:T(8,128)(2,1)} %param.6, pred[32,8,32,128]{3,2,1,0:T(32,128)(4,1)S(1)} %bitcast.12), kind=kOutput, calls=%fused_computation.19 | convolution fusion | flops 1616903936 | bytes 9865216 | tf_op jit(solution)/shard_map/dot_general | solution.py:17
  151.3 0.0 slice-done
  151.3 0.0 slice-done.1
  151.4 2.7 fusion.4
  154.1 0.0 all-reduce.2.cloned.1.call-update
  154.1 140.7 %psum.23 = f32[256]{0:T(256)S(1)} all-reduce(f32[256]{0:T(256)S(1)} %get-tuple-element.5), channel_id=1, replica_groups=mesh['bank'=8,'gal'=64] {'gal'}, use_global_device_ids=true, to_apply=%region_8.9 | all-reduce | flops 256 | bytes 2048 | tf_op jit(solution)/shard_map/psum | solution.py:55
  294.8 0.1 dynamic_slice.7
  294.9 14.5 %all-reduce.2.cloned.1.call-done = f32[256,768]{1,0:T(8,128)} async-done(((f32[256,768]{1,0:T(8,128)}), f32[256,768]{1,0:T(8,128)}) %all-reduce.2.cloned.1.call-update) | async-done | bytes 786448 | tf_op jit(solution)/shard_map/psum | solution.py:55
  309.4 1.4 dynamic-slice_divide_fusion
  (7 shorter events, 0.1 us)
Async XLA Ops:
  6.5 4.2 %copy-start.1 = (s32[256,8]{0,1:T(8,128)S(1)}, s32[256,8]{0,1:T(8,128)}, u32[]{:S(2)}) copy-start(s32[256,8]{0,1:T(8,128)} %param.8) | copy-start | bytes 24580
  6.5 4.2 %copy-start.2 = (s32[256,8]{0,1:T(8,128)S(1)}, s32[256,8]{0,1:T(8,128)}, u32[]{:S(2)}) copy-start(s32[256,8]{0,1:T(8,128)} %param.9) | copy-start | bytes 24580
  6.5 4.4 %copy-start.3 = (bf16[4,768]{1,0:T(4,128)(2,1)S(1)}, bf16[4,768]{1,0:T(4,128)(2,1)}, u32[]{:S(2)}) copy-start(bf16[4,768]{1,0:T(4,128)(2,1)} %param.7) | copy-start | bytes 18436
  6.5 61.5 %copy-start = (bf16[8,768]{1,0:T(8,128)(2,1)S(1)}, bf16[8,768]{1,0:T(8,128)(2,1)}, u32[]{:S(2)}) copy-start(bf16[8,768]{1,0:T(8,128)(2,1)} %param.5) | copy-start | bytes 36868
  6.5 302.8 %all-reduce.2.cloned.1.call-start = ((), (), s32[]{:S(2)}) async-start(), calls=%async_computation | async-start | bytes 1572864 | tf_op jit(solution)/shard_map/psum | solution.py:55
  143.9 7.4 %slice-start = ((s8[6291456]{0:T(1024)(128)(4,1)}), s8[4194304]{0:T(1024)(128)(4,1)S(1)}, s32[]{:S(2)}) async-start(s8[6291456]{0:T(1024)(128)(4,1)} %bitcast.10), calls=%async_computation.1 | async-start | bytes 8388608
  146.0 5.3 %slice-start.1 = ((s8[6291456]{0:T(1024)(128)(4,1)}), s8[2097152]{0:T(1024)(128)(4,1)S(1)}, s32[]{:S(2)}) async-start(s8[6291456]{0:T(1024)(128)(4,1)} %bitcast.10), calls=%async_computation.2 | async-start | bytes 4194304
Sparse Core Ops, SparseCore 0:
  154.2 155.1 all-reduce.1
where the time goes:
time: 318 us
  blocking collectives  267 us (84%)
  matrix products  14.6 us (5%)
  waiting for transfers between devices  14.5 us (5%)
  between operations  13.5 us (4%)
  other arithmetic  5.96 us (2%)
    psum x1, blocking collectives, body(): numer_all, denom_all = lax.psum((numerator, denominator), 'gal')  141 us
    all_gather x1, blocking collectives, body(): queries = lax.all_gather(test_queries, 'gal', axis=0, tiled=True)  56.8 us
    all_gather x1, blocking collectives, body(): portion = lax.all_gather(bank_queries, 'gal', axis=0, tiled=True)  48.5 us
    psum x1, blocking collectives, body(): colsum = lax.psum(partial_sums, 'bank')  20.6 us
    psum x1, waiting for transfers between devices, body(): numer_all, denom_all = lax.psum((numerator, denominator), 'gal')  14.5 us
    dot_general x2, matrix products, inner_rows(): lax.dot_general(first_rows, second_rows, (((1,), (1,)), ((), ())), prefer...  11.8 us
  transfers between devices with their start and end apart: 1, of which 1 were waited for; matrix products, arithmetic and copies ran while one was open for 0% of the time, Pallas kernels for 0%

commit v1 on v0

--- a/solution.py
+++ b/solution.py
@@ -6,6 +6,12 @@
 BLOCK = 128
 SHARPNESS = 20.0
 epsilon = 1e-06
+
+
+def add_all(shard, axis):
+    parts = lax.all_gather(shard, axis, axis=0, tiled=False)
+    total = parts.sum(axis=0)
+    return total
 
 
 def row_scale(matrix):
@@ -30,7 +36,7 @@
         * gallery_scale[None, :]
     )
     partial_sums = jnp.sum(jnp.exp(scores), axis=0)
-    colsum = lax.psum(partial_sums, "bank")
+    colsum = add_all(partial_sums, "bank")
     log_col = jnp.log(colsum)
     own_rows = test_queries.shape[0]
     slab_index = lax.axis_index("gal")

time: 318 us -> 309 us (0.972)
  blocking collectives: 267 us -> 259 us
    psum x1 -> x0, blocking collectives: 20.6 us -> none  [body(): colsum = lax.psum(partial_sums, 'bank')]
    all_gather x0 -> x1, blocking collectives: none -> 12.8 us  [add_all(): parts = lax.all_gather(shard, axis, axis=0, tiled=False)]
where the time goes in v1:
time: 309 us
  blocking collectives  259 us (84%)
  matrix products  14.6 us (5%)
  waiting for transfers between devices  13.8 us (4%)
  between operations  13.6 us (4%)
  other arithmetic  6 us (2%)
    psum x1, blocking collectives, body(): numer_all, denom_all = lax.psum((numerator, denominator), 'gal')  141 us
    all_gather x1, blocking collectives, body(): queries = lax.all_gather(test_queries, 'gal', axis=0, tiled=True)  56.8 us
    all_gather x1, blocking collectives, body(): portion = lax.all_gather(bank_queries, 'gal', axis=0, tiled=True)  48.5 us
    psum x1, waiting for transfers between devices, body(): numer_all, denom_all = lax.psum((numerator, denominator), 'gal')  13.8 us
    all_gather x1, blocking collectives, add_all(): parts = lax.all_gather(shard, axis, axis=0, tiled=False)  12.8 us
    dot_general x2, matrix products, inner_rows(): lax.dot_general(first_rows, second_rows, (((1,), (1,)), ((), ())), prefer...  11.8 us
  transfers between devices with their start and end apart: 1, of which 1 were waited for; matrix products, arithmetic and copies ran while one was open for 0% of the time, Pallas kernels for 0%

profile of v1, /device:TPU:2, one launch (start us, length us, event | category | flops | bytes accessed | tf_op | source)
XLA Modules:
  0.0 309.1 jit_solution(16837567404909940524)
XLA Ops:
  6.5 0.0 copy-start.1
  6.5 0.0 copy-start.2
  6.5 0.0 copy-start.3
  6.5 0.0 copy-start
  6.5 0.0 all-reduce.2.cloned.1.call-start
  6.6 4.1 %multiply_reduce_fusion = f32[4096]{0:T(1024)S(1)} fusion(bf16[4096,768]{1,0:T(8,128)(2,1)} %param.6), kind=kLoop, calls=%fused_computation | loop fusion | flops 9433088 | bytes 6307840 | tf_op jit(solution)/shard_map/reduce_sum | solution.py:19
  10.7 0.0 copy-done.1
  10.7 0.0 copy-done.2
  10.8 0.1 copy.10
  10.9 0.0 copy-done.3
  10.9 56.8 %all-gather.1 = bf16[64,4,768]{2,1,0:T(4,128)(2,1)S(1)} all-gather(bf16[1,4,768]{2,1,0:T(4,128)(2,1)S(1)} %bitcast.13), channel_id=1, replica_groups=mesh['bank'=8,'gal'=64] {'gal'}, dimensions={0}, use_global_device_ids=true | all-gather | bytes 399360 | tf_op jit(solution)/shard_map/all_gather | solution.py:43
  67.7 0.1 reshape.24
  67.8 0.2 multiply_reduce_fusion.2
  68.0 0.0 copy-done
  68.0 48.5 %all_gather.13 = bf16[512,768]{1,0:T(8,128)(2,1)S(1)} all-gather(bf16[8,768]{1,0:T(8,128)(2,1)S(1)} %copy-done), channel_id=1, replica_groups=mesh['bank'=8,'gal'=64] {'gal'}, dimensions={0}, use_global_device_ids=true | all-gather | bytes 798720 | tf_op jit(solution)/shard_map/all_gather | solution.py:31
  116.5 0.2 multiply_reduce_fusion.1
  116.8 6.5 %exponential_reduce_fusion = f32[4096]{0:T(1024)S(1)} fusion(bf16[512,768]{1,0:T(8,128)(2,1)S(1)} %all_gather.13, bf16[4096,768]{1,0:T(8,128)(2,1)} %param.6, f32[4096]{0:T(1024)S(1)} %add_rsqrt_fusion, f32[512]{0:T(512)S(1)} %rsqrt_multiply_fusion), kind=kOutput, calls=%fused_computation.1 | convolution fusion | flops 3227512832 | bytes 7112704 | tf_op jit(solution)/shard_map/dot_general | solution.py:23
  123.3 12.8 %all-gather = f32[32768]{0:T(1024)S(1)} all-gather(f32[4096]{0:T(1024)S(1)} %exponential_reduce_fusion), channel_id=2, replica_groups=mesh['bank'=8,'gal'=64] {'bank'}, dimensions={0}, use_global_device_ids=true | all-gather | bytes 147456 | tf_op jit(solution)/shard_map/all_gather | solution.py:12
  136.2 0.0 slice-start
  136.2 2.1 broadcast_in_dim.5
  138.3 0.0 slice-start.1
  138.3 5.3 %fusion.8 = (f32[256]{0:T(256)S(1)}, bf16[256,4096]{1,0:T(8,128)(2,1)S(1)}) fusion(f32[4096]{0:T(1024)S(1)} %log.7, f32[4096]{0:T(1024)S(1)} %add_rsqrt_fusion, f32[256]{0:T(256)S(1)} %rsqrt_multiply_fusion.1, bf16[256,768]{1,0:T(8,128)(2,1)S(1)} %reshape.24, bf16[4096,768]{1,0:T(8,128)(2,1)} %param.6, pred[32,8,32,128]{3,2,1,0:T(32,128)(4,1)S(1)} %bitcast.12), kind=kOutput, calls=%fused_computation.19 | convolution fusion | flops 1616903936 | bytes 9865216 | tf_op jit(solution)/shard_map/dot_general | solution.py:23
  143.6 0.0 slice-done
  143.6 0.0 slice-done.1
  143.6 2.7 fusion.4
  146.3 0.0 all-reduce.2.cloned.1.call-update
  146.4 140.6 %psum.15 = f32[256]{0:T(256)S(1)} all-reduce(f32[256]{0:T(256)S(1)} %get-tuple-element.5), channel_id=1, replica_groups=mesh['bank'=8,'gal'=64] {'gal'}, use_global_device_ids=true, to_apply=%region_8.9 | all-reduce | flops 256 | bytes 2048 | tf_op jit(solution)/shard_map/psum | solution.py:61
  287.0 0.1 dynamic_slice.7
  287.1 13.8 %all-reduce.2.cloned.1.call-done = f32[256,768]{1,0:T(8,128)} async-done(((f32[256,768]{1,0:T(8,128)}), f32[256,768]{1,0:T(8,128)}) %all-reduce.2.cloned.1.call-update) | async-done | bytes 786448 | tf_op jit(solution)/shard_map/psum | solution.py:61
  300.8 1.4 dynamic-slice_divide_fusion
  (9 shorter events, 0.1 us)
Async XLA Ops:
  6.5 4.2 %copy-start.1 = (s32[256,8]{0,1:T(8,128)S(1)}, s32[256,8]{0,1:T(8,128)}, u32[]{:S(2)}) copy-start(s32[256,8]{0,1:T(8,128)} %param.8) | copy-start | bytes 24580
  6.5 4.2 %copy-start.2 = (s32[256,8]{0,1:T(8,128)S(1)}, s32[256,8]{0,1:T(8,128)}, u32[]{:S(2)}) copy-start(s32[256,8]{0,1:T(8,128)} %param.9) | copy-start | bytes 24580
  6.5 4.4 %copy-start.3 = (bf16[4,768]{1,0:T(4,128)(2,1)S(1)}, bf16[4,768]{1,0:T(4,128)(2,1)}, u32[]{:S(2)}) copy-start(bf16[4,768]{1,0:T(4,128)(2,1)} %param.7) | copy-start | bytes 18436
  6.5 61.5 %copy-start = (bf16[8,768]{1,0:T(8,128)(2,1)S(1)}, bf16[8,768]{1,0:T(8,128)(2,1)}, u32[]{:S(2)}) copy-start(bf16[8,768]{1,0:T(8,128)(2,1)} %param.5) | copy-start | bytes 36868
  6.5 294.3 %all-reduce.2.cloned.1.call-start = ((), (), s32[]{:S(2)}) async-start(), calls=%async_computation | async-start | bytes 1572864 | tf_op jit(solution)/shard_map/psum | solution.py:61
  136.2 7.4 %slice-start = ((s8[6291456]{0:T(1024)(128)(4,1)}), s8[4194304]{0:T(1024)(128)(4,1)S(1)}, s32[]{:S(2)}) async-start(s8[6291456]{0:T(1024)(128)(4,1)} %bitcast.10), calls=%async_computation.1 | async-start | bytes 8388608
  138.3 5.3 %slice-start.1 = ((s8[6291456]{0:T(1024)(128)(4,1)}), s8[2097152]{0:T(1024)(128)(4,1)S(1)}, s32[]{:S(2)}) async-start(s8[6291456]{0:T(1024)(128)(4,1)} %bitcast.10), calls=%async_computation.2 | async-start | bytes 4194304
Sparse Core Ops, SparseCore 0:
  146.5 154.3 all-reduce.1

commit v2 on v0

--- a/solution.py
+++ b/solution.py
@@ -6,6 +6,16 @@
 BLOCK = 128
 SHARPNESS = 20.0
 epsilon = 1e-06
+
+
+def _take_slabs(incoming_x, mesh_name="gal"):
+    f_now = lax.all_to_all(
+        jnp.stack([incoming_x] * lax.axis_size(mesh_name)),
+        axis_name=mesh_name,
+        split_axis=0,
+        concat_axis=0,
+    )
+    return jnp.concatenate(f_now, axis=0)
 
 
 def row_scale(matrix):
@@ -22,7 +32,7 @@
 def body(bank_queries, gallery, test_queries, test_slabs, test_offsets):
     gallery_rows = gallery.shape[0]
     gallery_scale = row_scale(gallery)
-    portion = lax.all_gather(bank_queries, "gal", axis=0, tiled=True)
+    portion = _take_slabs(bank_queries)
     scores = (
         SHARPNESS
         * inner_rows(portion, gallery)

time: 318 us -> 296 us (0.931)
  blocking collectives: 267 us -> 222 us
  starting transfers between devices: 0.03 us -> 16.6 us
  waiting for transfers between devices: 14.5 us -> 18 us
    all_gather x1 -> x0, blocking collectives: 48.5 us -> none  [body(): portion = lax.all_gather(bank_queries, 'gal', axis=0, tiled=True)]
    all_to_all x0 -> x1, starting transfers between devices: none -> 16.6 us  [_take_slabs(): lax.all_to_all(jnp.stack([incoming_x] * lax.axis_size(mesh_name)), axis_n...]
    all_gather x1, blocking collectives: 56.8 us -> 60.4 us  [body(): queries = lax.all_gather(test_queries, 'gal', axis=0, tiled=True)]
    psum x1, waiting for transfers between devices: 14.5 us -> 17.9 us  [body(): numer_all, denom_all = lax.psum((numerator, denominator), 'gal')]
  transfers between devices with their start and end apart: 1 -> 2, of which waited for: 1 -> 1; matrix products, arithmetic and copies ran while one was open for 0% -> 2% of each run, Pallas kernels for 0% -> 0%
where the time goes in v2:
time: 296 us
  blocking collectives  222 us (75%)
  waiting for transfers between devices  18 us (6%)
  starting transfers between devices  16.6 us (6%)
  matrix products  14.5 us (5%)
  between operations  13.5 us (5%)
  other arithmetic  7.36 us (2%)
  local copies, waits for them, and re-layouts  4.09 us (1%)
    psum x1, blocking collectives, body(): numer_all, denom_all = lax.psum((numerator, denominator), 'gal')  141 us
    all_gather x1, blocking collectives, body(): queries = lax.all_gather(test_queries, 'gal', axis=0, tiled=True)  60.4 us
    psum x1, blocking collectives, body(): colsum = lax.psum(partial_sums, 'bank')  20.6 us
    psum x1, waiting for transfers between devices, body(): numer_all, denom_all = lax.psum((numerator, denominator), 'gal')  17.9 us
    all_to_all x1, starting transfers between devices, _take_slabs(): lax.all_to_all(jnp.stack([incoming_x] * lax.axis_size(mesh_name)), axis_n...  16.6 us
    dot_general x2, matrix products, inner_rows(): lax.dot_general(first_rows, second_rows, (((1,), (1,)), ((), ())), prefer...  11.8 us
  transfers between devices with their start and end apart: 2, of which 1 were waited for; matrix products, arithmetic and copies ran while one was open for 2% of the time, Pallas kernels for 0%

profile of v2, /device:TPU:2, one launch (start us, length us, event | category | flops | bytes accessed | tf_op | source)
XLA Modules:
  0.0 295.7 jit_solution(6478085900478341852)
XLA Ops:
  6.5 1.6 stack.2
  8.2 16.6 %all-to-all-start = ((bf16[64,8,768]{2,1,0:T(8,128)(2,1)}), bf16[64,8,768]{2,1,0:T(8,128)(2,1)S(1)}, u32[]{:S(2)}, u32[]{:S(2)}) async-start(bf16[64,8,768]{2,1,0:T(8,128)(2,1)} %stack.2), calls=%async_computation | async-start | bytes 1572864 | tf_op jit(solution)/shard_map/all_to_all | solution.py:12
  24.8 0.0 all-reduce.2.cloned.1.call-start
  24.8 0.7 broadcast_compare_fusion
  25.5 0.7 fusion.8
  26.3 0.1 copy.12
  26.4 60.4 %all-gather = bf16[64,4,768]{2,1,0:T(4,128)(2,1)S(1)} all-gather(bf16[1,4,768]{2,1,0:T(4,128)(2,1)} %bitcast.15), channel_id=1, replica_groups=mesh['bank'=8,'gal'=64] {'gal'}, dimensions={0}, use_global_device_ids=true | all-gather | bytes 399360 | tf_op jit(solution)/shard_map/all_gather | solution.py:47
  86.8 0.1 reshape.36
  86.9 0.2 multiply_reduce_fusion.2
  87.1 4.1 %multiply_reduce_fusion = f32[4096]{0:T(1024)S(1)} fusion(bf16[4096,768]{1,0:T(8,128)(2,1)} %param.6), kind=kLoop, calls=%fused_computation | loop fusion | flops 9433088 | bytes 6307840 | tf_op jit(solution)/shard_map/reduce_sum | solution.py:23
  91.2 0.0 all-to-all-done
  91.2 0.2 multiply_reduce_fusion.1
  91.4 0.1 mul.70
  91.5 6.5 %exponential_reduce_fusion = f32[4096]{0:T(1024)S(1)} fusion(bf16[4096,768]{1,0:T(8,128)(2,1)} %param.6, f32[4096]{0:T(1024)S(1)} %add_rsqrt_fusion, f32[512]{0:T(512)S(1)} %mul.70, bf16[64,8,768]{2,1,0:T(8,128)(2,1)S(1)} %all-to-all-done), kind=kOutput, calls=%fused_computation.1 | convolution fusion | flops 3227512832 | bytes 7112704 | tf_op jit(solution)/shard_map/dot_general | solution.py:27
  98.1 20.6 %psum.21 = f32[4096]{0:T(1024)S(1)} all-reduce(f32[4096]{0:T(1024)S(1)} %exponential_reduce_fusion), channel_id=1, replica_groups=mesh['bank'=8,'gal'=64] {'bank'}, use_global_device_ids=true, to_apply=%region_5.0 | all-reduce | flops 4096 | bytes 32768 | tf_op jit(solution)/shard_map/psum | solution.py:43
  118.7 0.0 slice-start
  118.7 2.1 broadcast_in_dim.5
  120.8 0.0 slice-start.1
  120.8 5.3 %fusion.9 = (f32[256]{0:T(256)S(1)}, bf16[256,4096]{1,0:T(8,128)(2,1)S(1)}) fusion(f32[4096]{0:T(1024)S(1)} %log.3, f32[4096]{0:T(1024)S(1)} %add_rsqrt_fusion, f32[256]{0:T(256)S(1)} %rsqrt_multiply_fusion.1, bf16[256,768]{1,0:T(8,128)(2,1)S(1)} %reshape.36, bf16[4096,768]{1,0:T(8,128)(2,1)} %param.6, pred[32,8,32,128]{3,2,1,0:T(32,128)(4,1)S(1)} %bitcast.14), kind=kOutput, calls=%fused_computation.20 | convolution fusion | flops 1616903936 | bytes 9865216 | tf_op jit(solution)/shard_map/dot_general | solution.py:27
  126.0 0.0 slice-done
  126.1 0.0 slice-done.1
  126.1 2.7 fusion.4
  128.8 0.0 all-reduce.2.cloned.1.call-update
  128.8 140.6 %psum.23 = f32[256]{0:T(256)S(1)} all-reduce(f32[256]{0:T(256)S(1)} %get-tuple-element.5), channel_id=1, replica_groups=mesh['bank'=8,'gal'=64] {'gal'}, use_global_device_ids=true, to_apply=%region_8.9 | all-reduce | flops 256 | bytes 2048 | tf_op jit(solution)/shard_map/psum | solution.py:65
  269.4 0.1 dynamic_slice.7
  269.5 17.9 %all-reduce.2.cloned.1.call-done = f32[256,768]{1,0:T(8,128)} async-done(((f32[256,768]{1,0:T(8,128)}), f32[256,768]{1,0:T(8,128)}) %all-reduce.2.cloned.1.call-update) | async-done | bytes 786448 | tf_op jit(solution)/shard_map/psum | solution.py:65
  287.5 1.4 dynamic-slice_divide_fusion
  (5 shorter events, 0.0 us)
Async XLA Ops:
  8.2 83.0 %all-to-all-start = ((bf16[64,8,768]{2,1,0:T(8,128)(2,1)}), bf16[64,8,768]{2,1,0:T(8,128)(2,1)S(1)}, u32[]{:S(2)}, u32[]{:S(2)}) async-start(bf16[64,8,768]{2,1,0:T(8,128)(2,1)} %stack.2), calls=%async_computation | async-start | bytes 1572864 | tf_op jit(solution)/shard_map/all_to_all | solution.py:12
  24.8 262.7 %all-reduce.2.cloned.1.call-start = ((), (), s32[]{:S(2)}) async-start(), calls=%async_computation.1 | async-start | bytes 1572864 | tf_op jit(solution)/shard_map/psum | solution.py:65
  118.7 7.3 %slice-start = ((s8[6291456]{0:T(1024)(128)(4,1)}), s8[4194304]{0:T(1024)(128)(4,1)S(1)}, s32[]{:S(2)}) async-start(s8[6291456]{0:T(1024)(128)(4,1)} %bitcast.12), calls=%async_computation.2 | async-start | bytes 8388608
  120.8 5.3 %slice-start.1 = ((s8[6291456]{0:T(1024)(128)(4,1)}), s8[2097152]{0:T(1024)(128)(4,1)S(1)}, s32[]{:S(2)}) async-start(s8[6291456]{0:T(1024)(128)(4,1)} %bitcast.12), calls=%async_computation.3 | async-start | bytes 4194304
Sparse Core Ops, SparseCore 0:
  128.9 158.4 all-reduce.1
